TPU v7x, 32 devices: a whole 2x2x4 slice. The times are simulated.
32 devices in a mesh: batch: 8 (over z, x), chan: 4 (over y, core).
Axes of the slice: x: 2, y: 2, z: 4, core: 2. Of those that a mesh axis runs over, the one named last changes fastest.
Arguments:
- signal: float32 [1024, 32768], P('chan', 'batch'), may hold values from -6 to 6
- cotangent: float32 [1024, 32768], P('chan', 'batch'), may hold values from -6 to 6
- first_layer: float32 [33, 64], replicated, may hold values from -5 to 5
- second_layer: float32 [64, 1024], P(None, 'chan'), may hold values from -0.75 to 0.75
- decay_rate: float32 [1024], P('chan'), may hold values from 0.3 to 600
- skip_gain: float32 [1024], P('chan'), may hold values from -4 to 4
Outputs:
- input_grad: float32 [1024, 32768], P('chan', 'batch')
- first_grad: float32 [33, 64], replicated
- second_grad: float32 [64, 1024], P(None, 'chan')
- decay_grad: float32 [1024], P('chan')
- skip_grad: float32 [1024], P('chan')
All inputs are finite; a program needn't handle non-finite values.
Results may differ from a plain program's by a relative error of at most 0.0003.
Values sent between devices are 32-bit elements; how exact they have to be, the bound alone decides.
A program may use at most 256 MiB of HBM per device.

v0:
```python
import math

import jax
import jax.numpy as jnp
from jax import lax
from jax.sharding import PartitionSpec as P

ROWS = 256


precise = lax.Precision.HIGHEST
epsilon = 1e-06


def features(positions, length, band_count):
    band_index = jnp.arange(1, band_count + 1, dtype=jnp.int32)
    phase = (band_index[:, None] * positions[None, :] % length).astype(jnp.float32) * (
        2.0 * math.pi / length
    )
    linear = positions.astype(jnp.float32)[None, :] / length
    return jnp.concatenate([linear, jnp.cos(phase), jnp.sin(phase)], axis=0)


def make_filter(first_layer, columns, rates, positions, length):
    embed = features(positions, length, first_layer.shape[0] // 2)
    before = jnp.dot(first_layer.T, embed, precision=precise)
    basis = jnp.sin(before)
    fraction = positions.astype(jnp.float32) / length
    window = jnp.exp(-rates[:, None] * fraction[None, :])
    shaped = window * jnp.dot(columns.T, basis, precision=precise)
    return (embed, before, basis, fraction, window, shaped)


def dft_tables(rows):
    counter = jnp.arange(rows, dtype=jnp.int32)
    product = counter[:, None] * counter[None, :]
    angle = (product % rows).astype(jnp.float32) * (2.0 * math.pi / rows)
    twist = product.astype(jnp.float32) * (2.0 * math.pi / (rows * rows))
    return (jnp.cos(angle), jnp.sin(angle), jnp.cos(twist), jnp.sin(twist))


def right_product(values, matrix):
    return jnp.dot(values, matrix, precision=precise)


def forward(signal, tables):
    cos_rows, sin_rows, cos_twist, sin_twist = tables
    rows = cos_rows.shape[0]
    half = rows // 2
    blocks = signal.reshape(signal.shape[0], half, rows)
    first_re = jnp.einsum("cam,ak->ckm", blocks, cos_rows[:half], precision=precise)
    first_im = -jnp.einsum("cam,ak->ckm", blocks, sin_rows[:half], precision=precise)
    twist_re = first_re * cos_twist + first_im * sin_twist
    twist_im = first_im * cos_twist - first_re * sin_twist
    spec_re = right_product(twist_re, cos_rows) + right_product(twist_im, sin_rows)
    spec_im = right_product(twist_im, cos_rows) - right_product(twist_re, sin_rows)
    return (spec_re, spec_im)


def inverse(spec_re, spec_im, tables):
    cos_rows, sin_rows, cos_twist, sin_twist = tables
    rows = cos_rows.shape[0]
    half = rows // 2
    back_re = right_product(spec_re, cos_rows) - right_product(spec_im, sin_rows)
    back_im = right_product(spec_im, cos_rows) + right_product(spec_re, sin_rows)
    turn_re = back_re * cos_twist - back_im * sin_twist
    turn_im = back_im * cos_twist + back_re * sin_twist
    blocks = jnp.einsum("ak,ckm->cam", cos_rows[:half], turn_re, precision=precise) - jnp.einsum(
        "ak,ckm->cam", sin_rows[:half], turn_im, precision=precise
    )
    return blocks.reshape(blocks.shape[0], half * rows) / float(rows * rows)


def correlate(values, cotan, filt, tables):
    count = values.shape[0]
    every_re, every_im = forward(jnp.concatenate([values, cotan, filt], axis=0), tables)
    val_re, cot_re, filt_re = (every_re[:count], every_re[count : 2 * count], every_re[2 * count :])
    val_im, cot_im, filt_im = (every_im[:count], every_im[count : 2 * count], every_im[2 * count :])
    prod_re = jnp.concatenate(
        [filt_re * cot_re + filt_im * cot_im, val_re * cot_re + val_im * cot_im], axis=0
    )
    prod_im = jnp.concatenate(
        [filt_re * cot_im - filt_im * cot_re, val_re * cot_im - val_im * cot_re], axis=0
    )
    both = inverse(prod_re, prod_im, tables)
    return (both[:count], both[count:])


def local(signal, cotangent, first_layer, second_layer, decay_rate, skip_gain):
    groups = lax.axis_size("batch")
    place = lax.axis_index("batch")
    width_dev = signal.shape[0]
    local_len = signal.shape[1]
    length = local_len * groups
    factor = 1.0 / math.sqrt(length)
    tables = dft_tables(ROWS)
    narrow = width_dev // groups
    spread_val, spread_cot = (
        lax.all_to_all(signal, "batch", split_axis=0, concat_axis=1, tiled=True),
        lax.all_to_all(cotangent, "batch", split_axis=0, concat_axis=1, tiled=True),
    )
    positions = jnp.arange(length, dtype=jnp.int32)
    columns = lax.dynamic_slice_in_dim(second_layer, place * narrow, narrow, 1)
    rates = lax.dynamic_slice_in_dim(decay_rate, place * narrow, narrow, 0)
    gains = lax.dynamic_slice_in_dim(skip_gain, place * narrow, narrow, 0)
    embed, before, basis, fraction, window, shaped = make_filter(
        first_layer, columns, rates, positions, length
    )
    norms = jnp.sqrt(jnp.sum(shaped * shaped, axis=1, keepdims=True) + epsilon)
    filt = shaped / norms
    in_grad, filt_grad = correlate(spread_val, spread_cot, filt, tables)
    in_grad = in_grad + gains[:, None] * spread_cot
    dfilt = factor * filt_grad
    skip_part = factor * jnp.sum(spread_cot * spread_val, axis=1)
    project = jnp.sum(filt * dfilt, axis=1, keepdims=True)
    draw = (dfilt - filt * project) / norms
    decay_part = -jnp.sum(draw * shaped * fraction[None, :], axis=1)
    dmix = draw * window
    second_part = jnp.dot(basis, dmix.T, precision=precise)
    dbasis = jnp.dot(columns, dmix, precision=precise)
    input_grad = lax.all_to_all(in_grad, "batch", split_axis=1, concat_axis=0, tiled=True)
    second_grad, decay_grad, skip_grad = (
        lax.all_gather(second_part, "batch", axis=1, tiled=True),
        lax.all_gather(decay_part, "batch", axis=0, tiled=True),
        lax.all_gather(skip_part, "batch", axis=0, tiled=True),
    )
    first_part = jnp.dot(embed, (jnp.cos(before) * dbasis).T, precision=precise)
    first_grad = lax.psum(first_part, ("batch", "chan"))
    return (input_grad, first_grad, second_grad, decay_grad, skip_grad)


def solution(mesh):
    placed = (P("chan", "batch"), P("chan", "batch"), P(), P(None, "chan"), P("chan"), P("chan"))
    return jax.shard_map(
        local,
        mesh=mesh,
        in_specs=placed,
        out_specs=(P("chan", "batch"), P(), P(None, "chan"), P("chan"), P("chan")),
        check_vma=False,
    )
```

profile of v0, /device:TPU:14, one launch (start us, length us, event | category | flops | bytes accessed | tf_op | source)
XLA Modules:
  0.0 858.1 jit_solution(15045509538001463544)
XLA Ops:
  0.7 6.4 all-to-all-start.1
  7.1 0.1 convert_multiply_fusion.1
  7.2 0.9 fusion.64
  8.1 0.9 fusion.63
  9.1 0.6 dynamic_slice.11
  9.7 0.1 copy.76
  9.8 0.1 copy.77
  9.9 8.2 fusion.51
  18.2 41.3 %fusion.122 = (f32[32768,64]{0,1:T(8,128)S(1)}, f32[32768,64]{0,1:T(8,128)}) fusion(f32[33,64]{1,0:T(8,128)S(1)} %copy-done.20, f32[16,32768]{1,0:T(8,128)S(1)} %get-tuple-element.36, f32[16,32768]{1,0:T(8,128)S(1)} %get-tuple-element.35, f32[1,32768]{1,0:T(1,128)S(1)} %convert_multiply_fusion.1), kind=kOutput, calls=%fused_computation.148 | convolution fusion | flops 832634880 | bytes 21111040 | tf_op jit(solution)/shard_map/dot_general | solution.py:26
  59.5 3.2 copy-done.1
  62.7 6.4 multiply_reduce_fusion.3
  69.1 27.9 %all-to-all-done.1 = f32[8,32,4096]{2,1,0:T(8,128)} async-done(((f32[8,32,4096]{2,1,0:T(8,128)}), f32[8,32,4096]{2,1,0:T(8,128)}, u32[]{:S(2)}, u32[]{:S(2)}) %all-to-all-start.1) | async-done | bytes 4194336 | tf_op jit(solution)/shard_map/all_to_all | solution.py:100
  97.0 7.8 all-to-all-start
  104.8 2.5 broadcast_divide_fusion
  107.3 3.3 copy.121
  110.6 1.0 fusion.69
  111.6 1.0 fusion.68
  112.5 6.7 copy.75
  119.3 4.9 concatenate.20
  124.2 69.9 %all-to-all-done = f32[8,32,4096]{2,1,0:T(8,128)} async-done(((f32[8,32,4096]{2,1,0:T(8,128)}), f32[8,32,4096]{2,1,0:T(8,128)}, u32[]{:S(2)}, u32[]{:S(2)}) %all-to-all-start) | async-done | bytes 4194336 | tf_op jit(solution)/shard_map/all_to_all | solution.py:99
  194.1 6.6 copy.74
  200.7 4.9 concatenate.19
  205.6 2.8 constant_dynamic-update-slice_fusion.2
  208.4 0.6 copy-done.11
  209.0 0.7 constant_dynamic-update-slice_fusion.1
  209.8 0.5 copy-done.10
  210.3 0.6 constant_dynamic-update-slice_fusion
  211.0 23.7 %fusion.79 = f32[256,96,256]{2,0,1:T(8,128)} fusion(f32[96,128,256]{2,1,0:T(8,128)S(1)} %constant_dynamic-update-slice_fusion, f32[256,256]{0,1:T(8,128)S(1)} %fusion.68), kind=kOutput, calls=%fused_computation.97 | convolution fusion | flops 9663676416 | bytes 37879808 | tf_op jit(solution)/shard_map/cam,ak->ckm/dot_general | solution.py:52
  234.6 23.2 %fusion.78 = f32[256,96,256]{2,0,1:T(8,128)} fusion(f32[96,128,256]{2,1,0:T(8,128)S(1)} %constant_dynamic-update-slice_fusion, f32[256,256]{0,1:T(8,128)S(1)} %fusion.69), kind=kOutput, calls=%fused_computation.96 | convolution fusion | flops 9663676416 | bytes 37879808 | tf_op jit(solution)/shard_map/cam,ak->ckm/dot_general | solution.py:51
  257.9 35.4 %fusion = f32[96,256,256]{2,1,0:T(8,128)} fusion(f32[256,96,256]{2,0,1:T(8,128)} %fusion.78, f32[256,96,256]{2,0,1:T(8,128)} %fusion.79, f32[256,256]{1,0:T(8,128)S(1)} %copy.77, f32[256,256]{1,0:T(8,128)S(1)} %copy.76), kind=kOutput, calls=%fused_computation.2 | convolution fusion | flops 19353436160 | bytes 76021760 | tf_op jit(solution)/shard_map/dot_general | solution.py:43
  293.2 35.4 %fusion.2 = f32[96,256,256]{2,1,0:T(8,128)} fusion(f32[256,96,256]{2,0,1:T(8,128)} %fusion.78, f32[256,96,256]{2,0,1:T(8,128)} %fusion.79, f32[256,256]{1,0:T(8,128)S(1)} %copy.77, f32[256,256]{1,0:T(8,128)S(1)} %copy.76), kind=kOutput, calls=%fused_computation.4 | convolution fusion | flops 19353436160 | bytes 76021760 | tf_op jit(solution)/shard_map/dot_general | solution.py:43
  328.6 40.2 %fusion.29 = f32[96,256,256]{2,1,0:T(8,128)} fusion(f32[96,256,256]{2,1,0:T(8,128)} %fusion, f32[256,256]{1,0:T(8,128)S(1)} %copy.77, f32[256,96,256]{2,0,1:T(8,128)} %fusion.79, f32[256,96,256]{2,0,1:T(8,128)} %fusion.78, f32[256,256]{1,0:T(8,128)S(1)} %copy.76), kind=kOutput, calls=%fused_computation.39 | convolution fusion | flops 19359727616 | bytes 101187584 | tf_op jit(solution)/shard_map/dot_general | solution.py:43
  368.8 40.0 %fusion.26 = f32[96,256,256]{2,1,0:T(8,128)} fusion(f32[96,256,256]{2,1,0:T(8,128)} %fusion.2, f32[256,256]{1,0:T(8,128)S(1)} %copy.77, f32[256,96,256]{2,0,1:T(8,128)} %fusion.79, f32[256,96,256]{2,0,1:T(8,128)} %fusion.78, f32[256,256]{1,0:T(8,128)S(1)} %copy.76), kind=kOutput, calls=%fused_computation.38 | convolution fusion | flops 19359727616 | bytes 101187584 | tf_op jit(solution)/shard_map/dot_general | solution.py:43
  408.8 28.6 %multiply_add_fusion.2 = (f32[32,256,256]{2,1,0:T(8,128)}, f32[32,256,256]{2,1,0:T(8,128)}, f32[32,256,256]{2,1,0:T(8,128)}, f32[32,256,256]{2,1,0:T(8,128)}) fusion(f32[96,256,256]{2,1,0:T(8,128)} %fusion.29, f32[96,256,256]{2,1,0:T(8,128)} %fusion.26), kind=kLoop, calls=%fused_computation.36 | loop fusion | flops 25165824 | bytes 83886080 | tf_op jit(solution)/shard_map/add | solution.py:80
  437.4 22.3 %fusion.16 = f32[64,256,256]{2,1,0:T(8,128)} fusion(f32[32,256,256]{2,1,0:T(8,128)} %get-tuple-element.30, f32[32,256,256]{2,1,0:T(8,128)} %get-tuple-element.32), kind=kOutput, calls=%fused_computation.22 | convolution fusion | flops 12890013696 | bytes 33554432 | tf_op jit(solution)/shard_map/dot_general | solution.py:43
  459.7 22.0 %fusion.17 = f32[64,256,256]{2,1,0:T(8,128)} fusion(f32[32,256,256]{2,1,0:T(8,128)} %get-tuple-element.30, f32[32,256,256]{2,1,0:T(8,128)} %get-tuple-element.32), kind=kOutput, calls=%fused_computation.23 | convolution fusion | flops 12890013696 | bytes 33554432 | tf_op jit(solution)/shard_map/dot_general | solution.py:43
  481.8 4.9 copy.120
  486.7 1.2 copy-done.2
  487.9 22.8 %fusion.21 = f32[64,256,256]{2,1,0:T(8,128)} fusion(f32[64,256,256]{2,1,0:T(8,128)} %fusion.16, f32[32,256,256]{2,1,0:T(8,128)} %get-tuple-element.31, f32[32,256,256]{2,1,0:T(8,128)S(1)} %copy-done.2), kind=kOutput, calls=%fused_computation.27 | convolution fusion | flops 12894208000 | bytes 50331648 | tf_op jit(solution)/shard_map/dot_general | solution.py:43
  510.7 22.8 %fusion.20 = f32[64,256,256]{2,1,0:T(8,128)} fusion(f32[64,256,256]{2,1,0:T(8,128)} %fusion.17, f32[32,256,256]{2,1,0:T(8,128)} %get-tuple-element.31, f32[32,256,256]{2,1,0:T(8,128)S(1)} %copy-done.2), kind=kOutput, calls=%fused_computation.26 | convolution fusion | flops 12894208000 | bytes 50331648 | tf_op jit(solution)/shard_map/dot_general | solution.py:43
  533.5 34.8 %fusion.8 = f32[64,256,128]{2,1,0:T(8,128)} fusion(f32[64,256,256]{2,1,0:T(8,128)} %fusion.20, f32[64,256,256]{2,1,0:T(8,128)} %fusion.21, f32[256,256]{1,0:T(8,128)S(1)} %copy.77, f32[256,256]{1,0:T(8,128)S(1)} %copy.76, f32[256,256]{0,1:T(8,128)S(1)} %copy-done.19), kind=kOutput, calls=%fused_computation.14 | convolution fusion | flops 6455033856 | bytes 42598400 | tf_op jit(solution)/shard_map/ak,ckm->cam/dot_general | solution.py:68
  568.2 35.9 %multiply_bitcast_fusion = f32[64,128,256]{1,2,0:T(8,128)} fusion(f32[64,256,128]{2,1,0:T(8,128)} %fusion.8, f32[64,256,256]{2,1,0:T(8,128)} %fusion.21, f32[64,256,256]{2,1,0:T(8,128)} %fusion.20, f32[256,256]{1,0:T(8,128)S(1)} %copy.77, f32[256,256]{1,0:T(8,128)S(1)} %copy.76, f32[256,256]{0,1:T(8,128)S(1)} %copy-done.17), kind=kOutput, calls=%fused_computation.28 | convolution fusion | flops 6459228160 | bytes 50987008 | tf_op jit(solution)/shard_map/ak,ckm->cam/dot_general | solution.py:68
  604.1 7.9 slice_multiply_fusion
  612.0 5.5 copy.122
  617.5 3.9 multiply_add_fusion.5
  621.4 2.4 copy.127
  623.8 7.9 all-to-all-start.2
  631.7 0.6 dynamic-slice
  633.0 5.5 copy.123
  638.5 4.2 multiply_reduce_fusion.2
  642.7 0.4 copy-done.3
  643.1 1.3 copy-done.5
  644.4 1.5 multiply_reduce_fusion.1
  645.9 1.1 slice-done.1
  647.0 7.1 fusion.35
  654.1 87.1 %all_gather.9 = f32[64,256]{0,1:T(8,128)S(1)} all-gather(f32[64,32]{0,1:T(8,128)S(1)} %fusion.35), channel_id=1, replica_groups=mesh['batch'=8,'chan'=4] {'batch'}, dimensions={1}, use_global_device_ids=true | all-gather | bytes 73728 | tf_op jit(solution)/shard_map/all_gather | solution.py:123
  741.2 0.7 copy.96
  741.9 4.1 multiply_reduce_fusion
  746.1 0.3 negate_dynamic-update-slice_fusion
  746.5 18.2 %all-reduce.2 = (f32[256]{0:T(256)}, f32[256]{0:T(256)}) all-reduce(f32[256]{0:T(256)S(1)} %negate_dynamic-update-slice_fusion, f32[256]{0:T(256)S(1)} %multiply_dynamic-update-slice_fusion), channel_id=1, replica_groups=mesh['batch'=8,'chan'=4] {'batch'}, use_global_device_ids=true, to_apply=%add | all-reduce | flops 512 | bytes 4096
  764.7 37.2 %convolution_multiply_fusion = f32[64,32768]{1,0:T(8,128)S(1)} fusion(f32[32768,64]{0,1:T(8,128)} %get-tuple-element.38, f32[32,32768]{1,0:T(8,128)} %copy-done.4, f32[32768]{0:T(1024)S(1)} %copy-done.13, f32[32]{0:T(128)S(1)} %copy-done.22, f32[64,256]{1,0:T(8,128)S(1)} %copy-done, s32[]{:T(128)S(6)} %select_n.43), kind=kOutput, calls=%fused_computation | convolution fusion | flops 809500672 | bytes 21135876 | tf_op jit(solution)/shard_map/dot_general | solution.py:120
  802.0 6.7 fusion.33
  808.7 44.4 %psum.7 = f32[33,64]{1,0:T(8,128)} all-reduce(f32[33,64]{1,0:T(8,128)S(1)} %fusion.33), channel_id=1, replica_groups=mesh['batch'=8,'chan'=4] {'batch','chan'}, use_global_device_ids=true, to_apply=%region_2.3 | all-reduce | flops 2112 | bytes 16896 | tf_op jit(solution)/shard_map/psum | solution.py:128
  853.0 4.7 copy.133
  (64 shorter events, 0.3 us)
Async XLA Ops:
  0.6 62.0 %copy-start = (f32[64,256]{1,0:T(8,128)S(1)}, f32[64,256]{1,0:T(8,128)}, u32[]{:S(2)}) copy-start(f32[64,256]{1,0:T(8,128)} %param.9) | copy-start | bytes 196612
  0.6 8.3 copy-start.26
  0.7 8.4 copy-start.27
  0.7 17.5 %copy-start.20 = (f32[33,64]{1,0:T(8,128)S(1)}, f32[33,64]{1,0:T(8,128)}, u32[]{:S(2)}) copy-start(f32[33,64]{1,0:T(8,128)} %param.8) | copy-start | bytes 25348
  0.7 96.3 %all-to-all-start.1 = ((f32[8,32,4096]{2,1,0:T(8,128)}), f32[8,32,4096]{2,1,0:T(8,128)}, u32[]{:S(2)}, u32[]{:S(2)}) async-start(f32[8,32,4096]{2,1,0:T(8,128)} %bitcast.94), calls=%async_computation.1 | async-start | bytes 8388608 | tf_op jit(solution)/shard_map/all_to_all | solution.py:100
  7.1 52.4 %copy-start.12 = (f32[32768]{0:T(1024)}, f32[32768]{0:T(1024)S(1)}, u32[]{:S(2)}) copy-start(f32[32768]{0:T(1024)S(1)} %convert_multiply_fusion.2) | copy-start | bytes 393220
  7.2 52.2 %copy-start.14 = (f32[1,32768]{1,0:T(1,128)}, f32[1,32768]{1,0:T(1,128)S(1)}, u32[]{:S(2)}) copy-start(f32[1,32768]{1,0:T(1,128)S(1)} %convert_multiply_fusion.1) | copy-start | bytes 393220
  9.1 50.4 %copy-start.21 = (f32[32]{0:T(128)}, f32[32]{0:T(128)S(1)}, u32[]{:S(2)}) copy-start(f32[32]{0:T(128)S(1)} %dynamic-slice_negate_fusion) | copy-start | bytes 388
  18.1 41.3 %copy-start.6 = (f32[16,32768]{1,0:T(8,128)}, f32[16,32768]{1,0:T(8,128)S(1)}, u32[]{:S(2)}) copy-start(f32[16,32768]{1,0:T(8,128)S(1)} %get-tuple-element.35) | copy-start | bytes 6291460
  18.1 41.3 %copy-start.8 = (f32[16,32768]{1,0:T(8,128)}, f32[16,32768]{1,0:T(8,128)S(1)}, u32[]{:S(2)}) copy-start(f32[16,32768]{1,0:T(8,128)S(1)} %get-tuple-element.36) | copy-start | bytes 6291460
  59.4 3.2 copy-start.1
  69.1 38.2 %copy-start.23 = (f32[32]{0:T(128)}, f32[32]{0:T(128)S(1)}, u32[]{:S(2)}) copy-start(f32[32]{0:T(128)S(1)} %add_sqrt_fusion) | copy-start | bytes 388
  97.0 97.1 %all-to-all-start = ((f32[8,32,4096]{2,1,0:T(8,128)}), f32[8,32,4096]{2,1,0:T(8,128)}, u32[]{:S(2)}, u32[]{:S(2)}) async-start(f32[8,32,4096]{2,1,0:T(8,128)} %bitcast.95), calls=%async_computation | async-start | bytes 8388608 | tf_op jit(solution)/shard_map/all_to_all | solution.py:99
  111.5 123.1 %copy-start.16 = (f32[256,256]{0,1:T(8,128)}, f32[256,256]{0,1:T(8,128)S(1)}, u32[]{:S(2)}) copy-start(f32[256,256]{0,1:T(8,128)S(1)} %fusion.69) | copy-start | bytes 786436
  112.5 98.4 %copy-start.18 = (f32[256,256]{0,1:T(8,128)}, f32[256,256]{0,1:T(8,128)S(1)}, u32[]{:S(2)}) copy-start(f32[256,256]{0,1:T(8,128)S(1)} %fusion.68) | copy-start | bytes 786436
  205.6 3.4 copy-start.11
  205.6 4.7 copy-start.10
  481.8 6.2 copy-start.2
  510.7 22.8 %copy-start.19 = (f32[256,256]{0,1:T(8,128)S(1)}, f32[256,256]{0,1:T(8,128)}, u32[]{:S(2)}) copy-start(f32[256,256]{0,1:T(8,128)} %copy-done.18) | copy-start | bytes 786436
  533.5 34.8 %copy-start.17 = (f32[256,256]{0,1:T(8,128)S(1)}, f32[256,256]{0,1:T(8,128)}, u32[]{:S(2)}) copy-start(f32[256,256]{0,1:T(8,128)} %copy-done.16) | copy-start | bytes 786436
  612.0 5.5 copy-start.25
  621.4 10.3 %copy-start.28 = (u32[32]{0:T(128)S(1)}, u32[32]{0:T(128)}, u32[]{:S(2)}) copy-start(u32[32]{0:T(128)} %constant.63) | copy-start | bytes 388
  623.8 14.7 %copy-start.24 = (f32[32]{0:T(128)S(1)}, f32[32]{0:T(128)}, u32[]{:S(2)}) copy-start(f32[32]{0:T(128)} %copy-done.23) | copy-start | bytes 388
  623.8 229.3 %all-to-all-start.2 = ((f32[32,8,4096]{2,0,1:T(8,128)}), f32[32,8,4096]{2,0,1:T(8,128)}, u32[]{:S(2)}, u32[]{:S(2)}) async-start(f32[32,8,4096]{2,0,1:T(8,128)} %bitcast.86), calls=%async_computation.2 | async-start | bytes 8388608 | tf_op jit(solution)/shard_map/all_to_all | solution.py:121
  633.0 9.7 %copy-start.13 = (f32[32768]{0:T(1024)S(1)}, f32[32768]{0:T(1024)}, u32[]{:S(2)}) copy-start(f32[32768]{0:T(1024)} %copy-done.12) | copy-start | bytes 393220
  638.5 4.6 copy-start.3
  638.5 5.9 copy-start.5
  638.5 7.4 slice-start
  644.4 2.6 slice-start.1
  644.4 2.6 copy-start.22
  645.9 8.2 copy-start.4
  764.7 37.3 %copy-start.7 = (f32[16,32768]{1,0:T(8,128)S(1)}, f32[16,32768]{1,0:T(8,128)}, u32[]{:S(2)}) copy-start(f32[16,32768]{1,0:T(8,128)} %copy-done.6) | copy-start | bytes 6291460
  764.7 37.3 %copy-start.9 = (f32[16,32768]{1,0:T(8,128)S(1)}, f32[16,32768]{1,0:T(8,128)}, u32[]{:S(2)}) copy-start(f32[16,32768]{1,0:T(8,128)} %copy-done.8) | copy-start | bytes 6291460
  764.7 37.3 %copy-start.15 = (f32[1,32768]{1,0:T(1,128)S(1)}, f32[1,32768]{1,0:T(1,128)}, u32[]{:S(2)}) copy-start(f32[1,32768]{1,0:T(1,128)} %copy-done.14) | copy-start | bytes 393220
where the time goes:
time: 867 us; the launch traced here: 858 us
  matrix products  457 us (53%)
  blocking collectives  150 us (17%)
  waiting for transfers between devices  97.7 us (11%)
  other arithmetic  65.3 us (8%)
  local copies, waits for them, and re-layouts  64.1 us (7%)
  starting transfers between devices  22.1 us (3%)
    dot_general x8, matrix products, right_product(): return jnp.dot(values, matrix, precision=precise)  241 us
    all_gather x1, blocking collectives, local(): lax.all_gather(second_part, 'batch', axis=1, tiled=True)  87.1 us
    all_to_all x1, waiting for transfers between devices, local(): lax.all_to_all(signal, 'batch', split_axis=0, concat_axis=1, tiled=True)  69.9 us
    psum x1, blocking collectives, local(): first_grad = lax.psum(first_part, ('batch', 'chan'))  44.4 us
    dot_general x1, matrix products, make_filter(): before = jnp.dot(first_layer.T, embed, precision=precise)  41.3 us
    dot_general x1, matrix products, local(): dbasis = jnp.dot(columns, dmix, precision=precise)  37.2 us
    dot_general x1, matrix products, inverse(): jnp.einsum('ak,ckm->cam', cos_rows[:half], turn_re, precision=precise)  35.9 us
    dot_general x1, matrix products, inverse(): jnp.einsum('ak,ckm->cam', sin_rows[:half], turn_im, precision=precise)  34.8 us
  transfers between devices with their start and end apart: 3, of which 2 were waited for; matrix products, arithmetic and copies ran while one was open for 17% of the time, Pallas kernels for 0%

commit v1 on v0

v1 whole, which is shorter than its diff:
```python
import functools
import math

import jax
import jax.numpy as jnp
import numpy as np
from jax import lax
from jax.experimental import pallas as pl
from jax.experimental.pallas import tpu as pltpu
from jax.sharding import PartitionSpec as P

COLS = 256

exact = lax.Precision.HIGHEST
precise = lax.Precision.HIGH
epsilon = 1e-06


def sincos(x):
    turns = jnp.round(x * (2.0 / math.pi))
    r = x - turns * 1.5703125
    r = r - turns * 4.837512969970703125e-4
    r = r - turns * 7.549789948768648e-8
    sq = r * r
    sine = r + r * sq * (-1.6666654611e-1 + sq * (8.3321608736e-3 + sq * -1.9515295891e-4))
    cosine = 1.0 - 0.5 * sq + sq * sq * (
        4.166664568298827e-2 + sq * (-1.388731625493765e-3 + sq * 2.443315711809948e-5)
    )
    quadrant = turns.astype(jnp.int32) & 3
    odd = (quadrant & 1) == 1
    sin_value = jnp.where(odd, cosine, sine)
    cos_value = jnp.where(odd, sine, cosine)
    sin_value = jnp.where(quadrant >= 2, -sin_value, sin_value)
    cos_value = jnp.where((quadrant == 1) | (quadrant == 2), -cos_value, cos_value)
    return sin_value, cos_value


def features(positions, length, band_count):
    band_index = jnp.arange(1, band_count + 1, dtype=jnp.int32)
    phase = (band_index[:, None] * positions[None, :] % length).astype(jnp.float32) * (
        2.0 * math.pi / length
    )
    linear = positions.astype(jnp.float32)[None, :] / length
    sines, cosines = sincos(phase)
    return jnp.concatenate([linear, cosines, sines], axis=0)


def pair(matrix):
    high = matrix.astype(np.float32).astype(jnp.bfloat16)
    low = (matrix - high.astype(np.float64)).astype(np.float32).astype(jnp.bfloat16)
    return jnp.asarray(high), jnp.asarray(low)


def tables(rows, cols):
    r = np.arange(rows, dtype=np.float64)
    c = np.arange(cols, dtype=np.float64)
    first = 2.0 * np.pi * np.outer(r + 0.5, r) / (2 * rows)
    twist = 2.0 * np.pi * np.outer(r + 0.5, c) / (2 * rows * cols)
    angle = 2.0 * np.pi * (np.outer(c, c) % cols) / cols
    cos_c, sin_c = np.cos(angle), np.sin(angle)
    stage1 = np.concatenate([np.cos(first), -np.sin(first)], axis=0)
    stage2 = np.block([[cos_c, -sin_c], [sin_c, cos_c]])
    last = np.concatenate([np.cos(first.T), -np.sin(first.T)], axis=1) / (rows * cols)
    return (
        *pair(stage1),
        *pair(stage2),
        *pair(stage2.T.copy()),
        *pair(last),
        jnp.asarray(np.cos(twist), jnp.float32),
        jnp.asarray(np.sin(twist), jnp.float32),
    )


def split(x):
    high = x.astype(jnp.bfloat16)
    return high, (x - high.astype(jnp.float32)).astype(jnp.bfloat16)


def dot(a, b):
    return jnp.dot(a, b, preferred_element_type=jnp.float32)


def product(left, right):
    return dot(left[0], right[0]) + (dot(left[1], right[0]) + dot(left[0], right[1]))


def kernel(count, val, cot, filt, w1h, w1l, w2h, w2l, w3h, w3l, w4h, w4l, ct, st, out_in, out_filt):
    rows, cols = ct.shape
    cos_t, sin_t = ct[...], st[...]
    first = (w1h[...], w1l[...])
    for c in range(count):
        parts = []
        for ref in (val, cot, filt):
            t = product(first, split(ref[c]))
            re, im = t[:rows], t[rows:]
            parts.append(
                jnp.concatenate([re * cos_t + im * sin_t, im * cos_t - re * sin_t], axis=1)
            )
        spec = product(split(jnp.concatenate(parts, axis=0)), (w2h[...], w2l[...]))
        v_re, v_im = spec[:rows, :cols], spec[:rows, cols:]
        c_re, c_im = spec[rows : 2 * rows, :cols], spec[rows : 2 * rows, cols:]
        f_re, f_im = spec[2 * rows :, :cols], spec[2 * rows :, cols:]
        prods = jnp.concatenate(
            [
                jnp.concatenate([f_re * c_re + f_im * c_im, f_re * c_im - f_im * c_re], axis=1),
                jnp.concatenate([v_re * c_re + v_im * c_im, v_re * c_im - v_im * c_re], axis=1),
            ],
            axis=0,
        )
        back = product(split(prods), (w3h[...], w3l[...]))
        for i, out in enumerate((out_in, out_filt)):
            re, im = back[i * rows : (i + 1) * rows, :cols], back[i * rows : (i + 1) * rows, cols:]
            turn = jnp.concatenate([re * cos_t - im * sin_t, im * cos_t + re * sin_t], axis=0)
            out[c] = product((w4h[...], w4l[...]), split(turn))


def correlate(values, cotan, filt):
    channels, rows, cols = values.shape
    count = 2 if channels % 2 == 0 else 1
    tabs = tables(rows, cols)
    block = pl.BlockSpec((count, rows, cols), lambda i: (i, 0, 0))
    shape = jax.ShapeDtypeStruct(values.shape, jnp.float32)
    flops = 2 * 3 * channels * rows * cols * (5 * 2 * rows + 5 * 4 * cols)
    return pl.pallas_call(
        functools.partial(kernel, count),
        grid=(channels // count,),
        in_specs=[block] * 3 + [pl.BlockSpec(t.shape, lambda i: (0, 0)) for t in tabs],
        out_specs=[block, block],
        out_shape=[shape, shape],
        compiler_params=pltpu.CompilerParams(vmem_limit_bytes=56 * 1024 * 1024),
        cost_estimate=pl.CostEstimate(
            flops=flops, bytes_accessed=5 * 4 * values.size, transcendentals=0
        ),
        name="correlate",
    )(values, cotan, filt, *tabs)


def local(signal, cotangent, first_layer, second_layer, decay_rate, skip_gain):
    groups = lax.axis_size("batch")
    place = lax.axis_index("batch")
    width_dev, local_len = signal.shape
    length = local_len * groups
    cols = COLS
    factor = 1.0 / math.sqrt(length)
    narrow = width_dev // groups

    def spread(x):
        x = x.reshape(width_dev, local_len // cols, cols)
        return lax.all_to_all(x, "batch", split_axis=0, concat_axis=1, tiled=True)

    val, cot = spread(signal), spread(cotangent)
    positions = jnp.arange(length, dtype=jnp.int32)
    columns = lax.dynamic_slice_in_dim(second_layer, place * narrow, narrow, 1)
    rates = lax.dynamic_slice_in_dim(decay_rate, place * narrow, narrow, 0)
    gains = lax.dynamic_slice_in_dim(skip_gain, place * narrow, narrow, 0)
    embed = features(positions, length, first_layer.shape[0] // 2)
    before = jnp.dot(first_layer.T, embed, precision=exact)
    basis, slope = sincos(before)
    fraction = positions.astype(jnp.float32) / length
    window = jnp.exp(-rates[:, None] * fraction[None, :])
    shaped = window * jnp.dot(columns.T, basis, precision=precise)
    norms = jnp.sqrt(jnp.sum(shaped * shaped, axis=1, keepdims=True) + epsilon)
    filt = shaped / norms
    taps = filt + jnp.where(positions[None, :] == 0, gains[:, None], 0.0)
    in_grad, filt_grad = correlate(val, cot, taps.reshape(val.shape))
    input_grad = lax.all_to_all(in_grad, "batch", split_axis=1, concat_axis=0, tiled=True)
    input_grad = input_grad.reshape(width_dev, local_len)
    dfilt = factor * filt_grad.reshape(narrow, length)
    skip_part = factor * jnp.sum(cot * val, axis=(1, 2))
    project = jnp.sum(filt * dfilt, axis=1, keepdims=True)
    draw = (dfilt - filt * project) / norms
    decay_part = -jnp.sum(draw * shaped * fraction[None, :], axis=1)
    dmix = draw * window
    second_part = jnp.dot(basis, dmix.T, precision=precise)
    dbasis = jnp.dot(columns, dmix, precision=precise)
    first_part = jnp.dot(embed, (slope * dbasis).T, precision=precise)
    second_grad, decay_grad, skip_grad = (
        lax.all_gather(second_part, "batch", axis=1, tiled=True),
        lax.all_gather(decay_part, "batch", axis=0, tiled=True),
        lax.all_gather(skip_part, "batch", axis=0, tiled=True),
    )
    first_grad = lax.psum(first_part, ("batch", "chan"))
    return (input_grad, first_grad, second_grad, decay_grad, skip_grad)


def solution(mesh):
    placed = (P("chan", "batch"), P("chan", "batch"), P(), P(None, "chan"), P("chan"), P("chan"))
    return jax.shard_map(
        local,
        mesh=mesh,
        in_specs=placed,
        out_specs=(P("chan", "batch"), P(), P(None, "chan"), P("chan"), P("chan")),
        check_vma=False,
    )
```

time: 867 us -> 524 us (0.60)
  matrix products: 457 us -> 47.3 us
  Pallas kernels: 0 us -> 87.1 us
  other arithmetic: 65.3 us -> 17 us
  waiting for transfers between devices: 97.7 us -> 135 us
  local copies, waits for them, and re-layouts: 64.1 us -> 44.7 us
  blocking collectives: 150 us -> 159 us
    dot_general x15 -> x3, matrix products: 413 us -> 27.9 us  [the longest x1 19.2 us: local(): before = jnp.dot(first_layer.T, embed, precision=exact)]
    pallas_call x0 -> x1, Pallas kernels: none -> 87.1 us  [correlate(): pl.pallas_call(functools.partial(kernel, count), grid=(channels // count,...]
    all_to_all x2, waiting for transfers between devices: 97.7 us -> 135 us  [spread(): return lax.all_to_all(x, 'batch', split_axis=0, concat_axis=1, tiled=True)]
    add x2 -> x1, other arithmetic: 32.5 us -> 2.74 us  [local(): taps = filt + jnp.where(positions[None, :] == 0, gains[:, None], 0.0)]
    dot_general x1, matrix products: 37.2 us -> 15.5 us  [local(): dbasis = jnp.dot(columns, dmix, precision=precise)]
    concatenate x3 -> x0, local copies, waits for them, and re-layouts: 10.5 us -> none  [correlate(): jnp.concatenate([values, cotan, filt], axis=0)]
    cos x3 -> x0, other arithmetic: 10 us -> none  [the longest x1 8.2 us: features(): return jnp.concatenate([linear, jnp.cos(phase), jnp.sin(phase)], axis=0)]
    all_to_all x3 -> x2, local copies, waits for them, and re-layouts: 18.3 us -> 9.59 us  [spread(): return lax.all_to_all(x, 'batch', split_axis=0, concat_axis=1, tiled=True)]
  transfers between devices with their start and end apart: 3 -> 3, of which waited for: 2 -> 2; matrix products, arithmetic and copies ran while one was open for 17% -> 16% of each run, Pallas kernels for 0% -> 0%
where the time goes in v1:
time: 524 us; the launch traced here: 514 us
  blocking collectives  159 us (30%)
  waiting for transfers between devices  135 us (26%)
  Pallas kernels  87.1 us (17%)
  matrix products  47.3 us (9%)
  local copies, waits for them, and re-layouts  44.7 us (9%)
  starting transfers between devices  22.5 us (4%)
  other arithmetic  17 us (3%)
    all_to_all x2, waiting for transfers between devices, spread(): return lax.all_to_all(x, 'batch', split_axis=0, concat_axis=1, tiled=True)  135 us
    all_gather x1, blocking collectives, local(): lax.all_gather(second_part, 'batch', axis=1, tiled=True)  95.5 us
    pallas_call x1, Pallas kernels, correlate(): pl.pallas_call(functools.partial(kernel, count), grid=(channels // count,...  87.1 us
    psum x1, blocking collectives, local(): first_grad = lax.psum(first_part, ('batch', 'chan'))  44.7 us
    unnamed x33, local copies, waits for them, and re-layouts  23.8 us
    dot_general x1, matrix products, local(): before = jnp.dot(first_layer.T, embed, precision=exact)  19.2 us
    unnamed x1, blocking collectives  18.4 us
    dot_general x1, matrix products, local(): dbasis = jnp.dot(columns, dmix, precision=precise)  15.5 us
  transfers between devices with their start and end apart: 3, of which 2 were waited for; matrix products, arithmetic and copies ran while one was open for 16% of the time, Pallas kernels for 0%

profile of v1, /device:TPU:14, one launch (start us, length us, event | category | flops | bytes accessed | tf_op | source)
XLA Modules:
  0.0 514.3 jit_solution(4661517701150644483)
XLA Ops:
  0.6 0.0 copy-start
  0.6 6.0 %copy.32 = f32[32,8,16,256]{3,2,1,0:T(8,128)} copy(f32[32,8,16,256]{3,1,2,0:T(8,128)} %bitcast.38) | data formatting | bytes 8388608
  6.6 6.2 %all-to-all-start = ((f32[256,16,256]{2,1,0:T(8,128)}), f32[256,16,256]{2,1,0:T(8,128)}, u32[]{:S(2)}, u32[]{:S(2)}) async-start(f32[256,16,256]{2,1,0:T(8,128)} %bitcast.33), calls=%async_computation | async-start | bytes 8388608 | tf_op jit(solution)/shard_map/all_to_all | solution.py:149
  12.8 0.0 copy-start.5
  12.8 4.8 negate_select_fusion.3
  17.6 0.0 copy-done.5
  17.6 0.0 copy-start.7
  17.6 0.0 copy-start.8
  17.6 0.0 copy-start.6
  17.6 3.7 copy.33
  21.3 0.0 copy-done.7
  21.3 0.1 dynamic_slice.11
  21.3 0.0 copy-done.8
  21.3 0.1 dynamic-slice_negate_fusion
  21.4 0.1 convert_multiply_fusion
  21.6 0.0 copy-done.6
  21.6 19.2 %negate_select_fusion.1 = (f32[64,32768]{1,0:T(8,128)S(1)}, f32[64,32768]{1,0:T(8,128)}) fusion(f32[33,64]{1,0:T(8,128)S(1)} %copy-done.6, f32[16,32768]{1,0:T(8,128)} %get-tuple-element.29, f32[16,32768]{1,0:T(8,128)S(1)} %get-tuple-element.28, f32[1,32768]{1,0:T(1,128)S(1)} %convert_multiply_fusion), kind=kOutput, calls=%fused_computation.4 | convolution fusion | flops 901840896 | bytes 21111040 | tf_op jit(solution)/shard_map/dot_general | solution.py:157
  40.8 0.0 copy-start.2
  40.8 0.0 copy-done
  40.8 5.0 multiply_reduce_fusion.3
  45.8 0.0 copy-done.2
  45.9 56.9 %all-to-all-done = f32[256,16,256]{2,1,0:T(8,128)} async-done(((f32[256,16,256]{2,1,0:T(8,128)}), f32[256,16,256]{2,1,0:T(8,128)}, u32[]{:S(2)}, u32[]{:S(2)}) %all-to-all-start) | async-done | bytes 4194336 | tf_op jit(solution)/shard_map/all_to_all | solution.py:149
  102.7 8.1 %all-to-all-start.1 = ((f32[256,16,256]{2,1,0:T(8,128)}), f32[256,16,256]{2,1,0:T(8,128)}, u32[]{:S(2)}, u32[]{:S(2)}) async-start(f32[256,16,256]{2,1,0:T(8,128)} %bitcast.34), calls=%async_computation.1 | async-start | bytes 8388608 | tf_op jit(solution)/shard_map/all_to_all | solution.py:149
  110.8 2.7 select_add_fusion
  113.6 3.4 copy.34
  116.9 4.8 copy.27
  121.8 78.3 %all-to-all-done.1 = f32[256,16,256]{2,1,0:T(8,128)} async-done(((f32[256,16,256]{2,1,0:T(8,128)}), f32[256,16,256]{2,1,0:T(8,128)}, u32[]{:S(2)}, u32[]{:S(2)}) %all-to-all-start.1) | async-done | bytes 4194336 | tf_op jit(solution)/shard_map/all_to_all | solution.py:149
  200.0 4.7 copy.28
  204.8 87.1 %correlate.1 = (f32[32,128,256]{2,1,0:T(8,128)}, f32[32,128,256]{2,1,0:T(8,128)}) custom-call(f32[32,128,256]{2,1,0:T(8,128)} %bitcast.41, f32[32,128,256]{2,1,0:T(8,128)} %bitcast.42, f32[32,128,256]{2,1,0:T(8,128)} %bitcast.40, bf16[256,128]{1,0:T(8,128)(2,1)} %constant.31.clone.w1h, bf16[256,128]{1,0:T(8,128)(2,1)} %constant.32.clone.w1l, ...), custom_call_target="tpu_custom_call" | custom-call | flops 40265318400 | bytes 20971520 | tf_op jit(solution)/shard_map/correlate/pallas_call | solution.py:124
  291.9 6.6 %copy.29 = f32[32,128,256]{2,0,1:T(8,128)} copy(f32[32,128,256]{2,1,0:T(8,128)} %get-tuple-element.7) | data formatting | bytes 8388608 | tf_op jit(solution)/shard_map/correlate/pallas_call | solution.py:124
  298.5 0.0 copy-start.9
  298.5 8.3 %all-to-all-start.2 = ((f32[32,128,256]{2,0,1:T(8,128)}), f32[32,128,256]{2,0,1:T(8,128)}, u32[]{:S(2)}, u32[]{:S(2)}) async-start(f32[32,128,256]{2,0,1:T(8,128)} %copy.29), calls=%async_computation.2 | async-start | bytes 8388608 | tf_op jit(solution)/shard_map/all_to_all | solution.py:166
  306.8 0.0 copy-done.9
  306.8 0.6 dynamic-slice
  308.1 2.6 broadcast_multiply_fusion
  310.6 0.0 copy-start.1
  310.6 2.4 copy.36
  313.1 0.0 copy-done.1
  313.1 0.0 slice-start
  313.1 0.9 multiply_reduce_fusion.2
  314.0 0.0 slice-start.1
  314.0 1.5 multiply_reduce_fusion.1
  315.5 0.0 copy-start.3
  315.5 0.0 slice-done
  315.6 1.2 slice-done.1
  316.8 3.9 fusion.11
  320.7 0.0 copy-done.3
  320.7 95.5 %all_gather.9 = f32[64,256]{0,1:T(8,128)S(1)} all-gather(f32[64,32]{0,1:T(8,128)S(1)} %fusion.11), channel_id=1, replica_groups=mesh['batch'=8,'chan'=4] {'batch'}, dimensions={1}, use_global_device_ids=true | all-gather | bytes 73728 | tf_op jit(solution)/shard_map/all_gather | solution.py:178
  416.2 0.7 copy.31
  416.9 4.1 multiply_reduce_fusion
  421.0 0.1 multiply_dynamic-update-slice_fusion
  421.1 0.1 negate_dynamic-update-slice_fusion
  421.1 18.4 %all-reduce.2 = (f32[256]{0:T(256)}, f32[256]{0:T(256)}) all-reduce(f32[256]{0:T(256)S(1)} %negate_dynamic-update-slice_fusion, f32[256]{0:T(256)S(1)} %multiply_dynamic-update-slice_fusion), channel_id=1, replica_groups=mesh['batch'=8,'chan'=4] {'batch'}, use_global_device_ids=true, to_apply=%add | all-reduce | flops 512 | bytes 4096
  439.6 0.0 copy-start.4
  439.6 15.5 %convolution_multiply_fusion = f32[64,32768]{1,0:T(8,128)S(1)} fusion(f32[64,32768]{1,0:T(8,128)} %get-tuple-element.31, f32[32,32768]{1,0:T(8,128)} %copy-done.3, f32[32768]{0:T(1024)S(1)} %convert_multiply_fusion.1, f32[32]{0:T(128)S(1)} %dynamic-slice_negate_fusion, f32[64,256]{1,0:T(8,128)S(1)} %copy-done, s32[]{:T(128)S(6)} %select_n.44), kind=kOutput, calls=%fused_computation | convolution fusion | flops 480247808 | bytes 21135876 | tf_op jit(solution)/shard_map/dot_general | solution.py:175
  455.1 0.0 copy-done.4
  455.1 3.7 fusion.10
  458.7 44.7 %psum.7 = f32[33,64]{1,0:T(8,128)} all-reduce(f32[33,64]{1,0:T(8,128)S(1)} %fusion.10), channel_id=1, replica_groups=mesh['batch'=8,'chan'=4] {'batch','chan'}, use_global_device_ids=true, to_apply=%region_2.3 | all-reduce | flops 2112 | bytes 16896 | tf_op jit(solution)/shard_map/psum | solution.py:182
  503.4 0.0 all-to-all-done.2
  503.4 4.6 copy.30
  508.0 5.8 %copy.35 = f32[32,8,16,256]{3,1,2,0:T(8,128)} copy(f32[32,8,16,256]{3,2,1,0:T(8,128)S(1)} %bitcast.37) | data formatting | bytes 8388608
  (7 shorter events, 0.0 us)
Async XLA Ops:
  0.6 40.2 %copy-start = (f32[64,256]{1,0:T(8,128)S(1)}, f32[64,256]{1,0:T(8,128)}, u32[]{:S(2)}) copy-start(f32[64,256]{1,0:T(8,128)} %param.19) | copy-start | bytes 196612
  6.6 96.1 %all-to-all-start = ((f32[256,16,256]{2,1,0:T(8,128)}), f32[256,16,256]{2,1,0:T(8,128)}, u32[]{:S(2)}, u32[]{:S(2)}) async-start(f32[256,16,256]{2,1,0:T(8,128)} %bitcast.33), calls=%async_computation | async-start | bytes 8388608 | tf_op jit(solution)/shard_map/all_to_all | solution.py:149
  12.8 4.8 copy-start.5
  17.6 3.7 copy-start.7
  17.6 3.7 copy-start.8
  17.6 4.0 copy-start.6
  40.8 5.0 copy-start.2
  102.7 97.3 %all-to-all-start.1 = ((f32[256,16,256]{2,1,0:T(8,128)}), f32[256,16,256]{2,1,0:T(8,128)}, u32[]{:S(2)}, u32[]{:S(2)}) async-start(f32[256,16,256]{2,1,0:T(8,128)} %bitcast.34), calls=%async_computation.1 | async-start | bytes 8388608 | tf_op jit(solution)/shard_map/all_to_all | solution.py:149
  298.5 8.3 %copy-start.9 = (u32[32]{0:T(128)S(1)}, u32[32]{0:T(128)}, u32[]{:S(2)}) copy-start(u32[32]{0:T(128)} %constant.121) | copy-start | bytes 388
  298.5 204.9 %all-to-all-start.2 = ((f32[32,128,256]{2,0,1:T(8,128)}), f32[32,128,256]{2,0,1:T(8,128)}, u32[]{:S(2)}, u32[]{:S(2)}) async-start(f32[32,128,256]{2,0,1:T(8,128)} %copy.29), calls=%async_computation.2 | async-start | bytes 8388608 | tf_op jit(solution)/shard_map/all_to_all | solution.py:166
  310.6 2.4 copy-start.1
  313.1 2.5 slice-start
  314.0 2.8 slice-start.1
  315.5 5.2 %copy-start.3 = (f32[32,32768]{1,0:T(8,128)}, f32[32,32768]{1,0:T(8,128)S(1)}, u32[]{:S(2)}) copy-start(f32[32,32768]{1,0:T(8,128)S(1)} %get-tuple-element.27) | copy-start | bytes 12582916
  439.6 15.5 %copy-start.4 = (f32[16,32768]{1,0:T(8,128)S(1)}, f32[16,32768]{1,0:T(8,128)}, u32[]{:S(2)}) copy-start(f32[16,32768]{1,0:T(8,128)} %get-tuple-element.29) | copy-start | bytes 6291460
